TPU v7x, 512 devices: a whole 4x8x8 slice. The times are simulated.
512 devices in a mesh: rows: 64 (over y, x, core), cols: 8 (over z).
Axes of the slice: x: 4, y: 8, z: 8, core: 2. Of those that a mesh axis runs over, the one named last changes fastest.
Arguments:
- fact_cells: bfloat16 [3072, 32, 512], P('rows', 'cols'), may hold values from -6 to 6
- gain_col: float32 [512], replicated, may hold values from 0.1 to 1.9
- w_qkv: bfloat16 [512, 1536], replicated, may hold values from -0.25 to 0.25
- w_col_out: bfloat16 [512, 512], replicated, may hold values from -0.25 to 0.25
- gain_tile: float32 [512], replicated, may hold values from 0.1 to 1.9
- w_query: bfloat16 [512, 512], replicated, may hold values from -0.25 to 0.25
- w_tile_out: bfloat16 [512, 512], replicated, may hold values from -0.25 to 0.25
- tile_kv: bfloat16 [256, 128, 8, 128], P('rows', None, 'cols'), may hold values from -70 to 70
- tile_ids: int32 [64, 48], P('rows'), may hold values from -1 to 255, as said below
- key_mask: int32 [3072, 48], P('rows'), may hold values from 0 to 1, as said below
Outputs:
- layer_out: bfloat16 [3072, 32, 512], P('rows', 'cols')
Inputs may be any that keep to these rules, and one draw needn't show every extreme that they name: `tile_ids`: tile t is held by index t // 4 of rows. In every block the first slots, 36 of them or more, hold distinct tile ids and the rest hold -1; some block fills all 48 slots. The listed tiles of one block are held by distinct indices of rows. `key_mask`: 0 wherever the row's block holds -1 in that slot; 1 in slot 0 of every row.
All inputs are finite; a program needn't handle non-finite values.
Results may differ from a plain program's by a relative error of at most 0.023.
The roundings to bfloat16 on the way count: a program that leaves them out, or rounds other values in their place, can miss the bound.
Values may be sent and summed in bfloat16 or wider, within the bound.
A program may use at most 64 MiB of HBM per device.

v0:
```python
import jax
import jax.numpy as jnp
from jax import lax
from jax.sharding import PartitionSpec as P


def rms_scale(values, gain_vec):
    mean_sq = jnp.mean(values * values, axis=-1, keepdims=True)
    return values * lax.rsqrt(mean_sq + 1e-05) * gain_vec


def soft_weights(scores, axes):
    row_top = jnp.max(scores, axis=axes, keepdims=True)
    expo_vals = jnp.exp(scores - row_top)
    return (expo_vals / jnp.sum(expo_vals, axis=axes, keepdims=True)).astype(jnp.bfloat16)


def column_attend(queries, keyvals, head_size):
    key_part = keyvals[..., :head_size]
    val_part = keyvals[..., head_size:]
    scores = jnp.einsum(
        "rchd,rkhd->rhck", queries, key_part, preferred_element_type=jnp.float32
    ) * head_size ** (-0.5)
    col_weights = soft_weights(scores, (3,))
    return jnp.einsum(
        "rhck,rkhd->rchd", col_weights, val_part, preferred_element_type=jnp.float32
    ).astype(jnp.bfloat16)


def tile_attend(queries, fetched, key_mask, head_size):
    key_part = fetched[..., :head_size]
    val_part = fetched[..., head_size:]
    row_count, col_count, head_count = queries.shape[:3]
    q_blocks = queries.reshape(row_count // 4, 4, col_count, head_count, head_size)
    m_blocks = key_mask.reshape(row_count // 4, 4, key_mask.shape[1])

    def one_block(block_pair):
        block_q, block_m = block_pair
        scores = jnp.einsum(
            "rchd,tkhd->rchtk", block_q, key_part, preferred_element_type=jnp.float32
        ) * head_size ** (-0.5)
        live_keys = (block_m > 0)[:, None, None, :, None]
        scores = jnp.where(live_keys, scores, -1e30)
        tile_weights = soft_weights(scores, (3, 4))
        return jnp.einsum(
            "rchtk,tkhd->rchd", tile_weights, val_part, preferred_element_type=jnp.float32
        ).astype(jnp.bfloat16)

    answer = lax.map(one_block, (q_blocks, m_blocks))
    return answer.reshape(row_count, col_count, head_count, head_size)


def fetch_all(tile_kv, tile_ids):
    gathered = lax.all_gather(tile_kv, "rows", axis=0, tiled=True)
    return jnp.take(gathered, jnp.maximum(tile_ids[0], 0), axis=0)


def project(normed, weight):
    return jnp.dot(normed.reshape(-1, weight.shape[0]), weight, preferred_element_type=jnp.float32)


def shards(
    fact_cells,
    gain_col,
    w_qkv,
    w_col_out,
    gain_tile,
    w_query,
    w_tile_out,
    tile_kv,
    tile_ids,
    key_mask,
):
    model_width = fact_cells.shape[2]
    head_size = tile_kv.shape[3] // 2
    heads_all = model_width // head_size
    fetched = fetch_all(tile_kv, tile_ids)
    row_count, col_local = (fact_cells.shape[0], fact_cells.shape[1])
    residual = fact_cells.astype(jnp.float32)
    normed = rms_scale(residual, gain_col).astype(jnp.bfloat16)
    packed = (
        project(normed, w_qkv)
        .astype(jnp.bfloat16)
        .reshape(row_count, col_local, 3, heads_all, head_size)
    )
    queries = packed[:, :, 0]
    keyvals = jnp.concatenate([packed[:, :, 1], packed[:, :, 2]], axis=-1)
    queries_h, keyvals_h = (
        lax.all_to_all(queries, "cols", split_axis=2, concat_axis=1, tiled=True),
        lax.all_to_all(keyvals, "cols", split_axis=2, concat_axis=1, tiled=True),
    )
    mixed_col = column_attend(queries_h, keyvals_h, head_size)
    mixed_back = lax.all_to_all(mixed_col, "cols", split_axis=1, concat_axis=2, tiled=True)
    residual = residual + project(mixed_back, w_col_out).reshape(residual.shape)
    normed2 = rms_scale(residual, gain_tile).astype(jnp.bfloat16)
    asked_q = (
        project(normed2, w_query)
        .astype(jnp.bfloat16)
        .reshape(row_count, col_local, heads_all, head_size)
    )
    asked_h = lax.all_to_all(asked_q, "cols", split_axis=2, concat_axis=1, tiled=True)
    answer = tile_attend(asked_h, fetched, key_mask, head_size)
    answer_back = lax.all_to_all(answer, "cols", split_axis=1, concat_axis=2, tiled=True)
    final_out = residual + project(answer_back, w_tile_out).reshape(residual.shape)
    return final_out.astype(jnp.bfloat16)


def solution(mesh):
    placed = (
        P("rows", "cols", None),
        P(),
        P(),
        P(),
        P(),
        P(),
        P(),
        P("rows", None, "cols", None),
        P("rows", None),
        P("rows", None),
    )
    return jax.shard_map(
        shards, mesh=mesh, in_specs=placed, out_specs=P("rows", "cols", None), check_vma=False
    )
```

profile of v0, /device:TPU:8, one launch (start us, length us, event | category | flops | bytes accessed | tf_op | source)
XLA Modules:
  0.0 198.4 jit_solution(1383678545264350636)
XLA Ops:
  7.3 1.1 fusion.30
  8.3 1.1 fusion.32
  11.1 1.0 reshape.174
  12.1 10.3 %all-to-all-start.1 = ((bf16[8,2,6144]{2,1,0:T(2,128)(2,1)}), bf16[8,2,6144]{2,1,0:T(2,128)(2,1)S(1)}, u32[]{:S(2)}, u32[]{:S(2)}) async-start(bf16[8,2,6144]{2,1,0:T(2,128)(2,1)} %reshape.174), calls=%async_computation.1 | async-start | bytes 393216 | tf_op jit(solution)/shard_map/all_to_all | solution.py:89
  22.8 1.3 pad_maximum_fusion
  24.2 8.8 %all-to-all-done.1 = bf16[8,2,6144]{2,1,0:T(2,128)(2,1)S(1)} async-done(((bf16[8,2,6144]{2,1,0:T(2,128)(2,1)}), bf16[8,2,6144]{2,1,0:T(2,128)(2,1)S(1)}, u32[]{:S(2)}, u32[]{:S(2)}) %all-to-all-start.1) | async-done | bytes 196640 | tf_op jit(solution)/shard_map/all_to_all | solution.py:89
  32.9 3.5 %all-to-all-start = ((bf16[48,4,8,128]{3,1,0,2:T(4,128)(2,1)}), bf16[48,4,8,128]{3,1,0,2:T(4,128)(2,1)S(1)}, u32[]{:S(2)}, u32[]{:S(2)}) async-start(bf16[48,4,8,128]{3,1,0,2:T(4,128)(2,1)} %pad_maximum_fusion), calls=%async_computation | async-start | bytes 786432 | tf_op jit(solution)/shard_map/all_to_all | solution.py:90
  37.0 12.4 %all-to-all-done = bf16[48,4,8,128]{3,1,0,2:T(4,128)(2,1)S(1)} async-done(((bf16[48,4,8,128]{3,1,0,2:T(4,128)(2,1)}), bf16[48,4,8,128]{3,1,0,2:T(4,128)(2,1)S(1)}, u32[]{:S(2)}, u32[]{:S(2)}) %all-to-all-start) | async-done | bytes 393248 | tf_op jit(solution)/shard_map/all_to_all | solution.py:90
  49.5 1.3 fusion.38
  50.8 1.6 fusion.26
  52.9 12.2 %all_to_all.78 = bf16[8,2,6144]{2,1,0:T(2,128)(2,1)S(1)} all-to-all(bf16[8,2,6144]{2,1,0:T(2,128)(2,1)S(1)} %reshape.176), channel_id=1, replica_groups=mesh['rows'=64,'cols'=8] {'cols'}, dimensions={0} | all-to-all | bytes 393216 | tf_op jit(solution)/shard_map/all_to_all | solution.py:93
  66.7 1.3 convolution_convert_fusion.2
  68.4 1.0 reshape.178
  69.3 3.6 %all-to-all-start.3 = ((bf16[8,2,6144]{2,1,0:T(2,128)(2,1)}), bf16[8,2,6144]{2,1,0:T(2,128)(2,1)S(1)}, u32[]{:S(2)}, u32[]{:S(2)}) async-start(bf16[8,2,6144]{2,1,0:T(2,128)(2,1)} %reshape.178), calls=%async_computation.3 | async-start | bytes 393216 | tf_op jit(solution)/shard_map/all_to_all | solution.py:101
  73.0 9.4 %all-to-all-done.3 = bf16[8,2,6144]{2,1,0:T(2,128)(2,1)S(1)} async-done(((bf16[8,2,6144]{2,1,0:T(2,128)(2,1)}), bf16[8,2,6144]{2,1,0:T(2,128)(2,1)S(1)}, u32[]{:S(2)}, u32[]{:S(2)}) %all-to-all-start.3) | async-done | bytes 196640 | tf_op jit(solution)/shard_map/all_to_all | solution.py:101
  83.8 20.0 %all-gather.2.cloned.1.call-done = bf16[256,128,1,128]{3,1,2,0:T(8,128)(2,1)} async-done(((bf16[4,128,1,128]{3,1,2,0:T(8,128)(2,1)}), bf16[256,128,1,128]{3,1,2,0:T(8,128)(2,1)}) %all-gather.2.cloned.1.call-update) | async-done | bytes 8388624 | tf_op jit(solution)/shard_map/all_gather | solution.py:54
  103.8 4.2 %gather_fusion = bf16[48,128,128]{2,1,0:T(8,128)(2,1)S(1)} fusion(bf16[256,128,128]{2,1,0:T(8,128)(2,1)} %bitcast.194, s32[1024]{0:T(1024)S(1)} %pad_clamp_fusion), kind=kCustom, calls=%fused_computation | custom fusion | bytes 3145920 | tf_op jit(solution)/shard_map/jit(_take)/gather | solution.py:55
  108.3 1.9 fusion.36
  110.1 1.4 copy.66
  111.6 1.7 copy.65
  113.3 56.9 %while.10 = (s32[]{:T(128)}, bf16[12,4,32,1,64]{4,1,0,2,3:T(4,128)(2,1)}, s32[12,4,48]{2,1,0:T(4,128)}, bf16[12,4,32,1,64]{4,2,1,3,0:T(8,128)(2,1)}, bf16[48,128...) while((s32[]{:T(128)}, bf16[12,4,32,1,64]{4,1,0,2,3:T(4,128)(2,1)}, ...), condition=%wide.region_7.8_spmd, body=%wide.region_4.0_spmd.sunk | while | flops 210771904 | bytes 14258301 | solution.py:49
  114.0 1.5 fusion.56
  115.5 0.9 fusion.57
  116.5 1.0 fusion.58
  118.8 1.5 fusion.56
  121.2 1.0 fusion.58
  123.5 1.5 fusion.56
  125.9 1.0 fusion.58
  128.2 1.5 fusion.56
  130.7 1.0 fusion.58
  133.0 1.5 fusion.56
  135.4 1.0 fusion.58
  137.7 1.5 fusion.56
  140.1 1.0 fusion.58
  142.4 1.5 fusion.56
  144.9 1.0 fusion.58
  147.2 1.5 fusion.56
  149.6 1.0 fusion.58
  151.9 1.5 fusion.56
  154.4 1.0 fusion.58
  156.7 1.5 fusion.56
  159.1 1.0 fusion.58
  161.4 1.5 fusion.56
  163.9 1.0 fusion.58
  166.2 1.5 fusion.56
  168.6 1.0 fusion.58
  170.2 1.4 reshape.180
  171.6 18.1 %all_to_all.79 = bf16[8,2,6144]{2,1,0:T(2,128)(2,1)S(1)} all-to-all(bf16[8,2,6144]{2,1,0:T(2,128)(2,1)S(1)} %reshape.180), channel_id=1, replica_groups=mesh['rows'=64,'cols'=8] {'cols'}, dimensions={0} | all-to-all | bytes 393216 | tf_op jit(solution)/shard_map/all_to_all | solution.py:103
  (110 shorter events, 35.7 us)
Async XLA Ops:
  6.5 3.1 %copy-start = (bf16[512,1536]{1,0:T(8,128)(2,1)S(1)}, bf16[512,1536]{1,0:T(8,128)(2,1)}, u32[]{:S(2)}) copy-start(bf16[512,1536]{1,0:T(8,128)(2,1)} %param.14) | copy-start | bytes 4718596
  6.5 97.3 %all-gather.2.cloned.1.call-start = ((), (), s32[]{:S(2)}) async-start(), calls=%async_computation.5 | async-start | bytes 8519680 | tf_op jit(solution)/shard_map/all_gather | solution.py:54
  12.1 20.8 %all-to-all-start.1 = ((bf16[8,2,6144]{2,1,0:T(2,128)(2,1)}), bf16[8,2,6144]{2,1,0:T(2,128)(2,1)S(1)}, u32[]{:S(2)}, u32[]{:S(2)}) async-start(bf16[8,2,6144]{2,1,0:T(2,128)(2,1)} %reshape.174), calls=%async_computation.1 | async-start | bytes 393216 | tf_op jit(solution)/shard_map/all_to_all | solution.py:89
  32.9 16.4 %all-to-all-start = ((bf16[48,4,8,128]{3,1,0,2:T(4,128)(2,1)}), bf16[48,4,8,128]{3,1,0,2:T(4,128)(2,1)S(1)}, u32[]{:S(2)}, u32[]{:S(2)}) async-start(bf16[48,4,8,128]{3,1,0,2:T(4,128)(2,1)} %pad_maximum_fusion), calls=%async_computation | async-start | bytes 786432 | tf_op jit(solution)/shard_map/all_to_all | solution.py:90
  50.8 15.1 %copy-start.1 = (bf16[48,4,512]{2,1,0:T(4,128)(2,1)S(1)}, bf16[48,4,512]{2,1,0:T(4,128)(2,1)}, u32[]{:S(2)}) copy-start(bf16[48,4,512]{2,1,0:T(4,128)(2,1)} %param.12) | copy-start | bytes 589828
  50.8 15.1 %copy-start.3 = (bf16[512,512]{1,0:T(8,128)(2,1)S(1)}, bf16[512,512]{1,0:T(8,128)(2,1)}, u32[]{:S(2)}) copy-start(bf16[512,512]{1,0:T(8,128)(2,1)} %param.15) | copy-start | bytes 1572868
  52.4 13.9 %copy-start.5 = (f32[512]{0:T(512)S(1)}, f32[512]{0:T(512)}, u32[]{:S(2)}) copy-start(f32[512]{0:T(512)} %param.16) | copy-start | bytes 6148
  65.7 7.3 %copy-start.6 = (s32[1,48]{1,0:T(1,128)S(1)}, s32[1,48]{1,0:T(1,128)}, u32[]{:S(2)}) copy-start(s32[1,48]{1,0:T(1,128)} %param.20) | copy-start | bytes 580
  69.3 13.1 %all-to-all-start.3 = ((bf16[8,2,6144]{2,1,0:T(2,128)(2,1)}), bf16[8,2,6144]{2,1,0:T(2,128)(2,1)S(1)}, u32[]{:S(2)}, u32[]{:S(2)}) async-start(bf16[8,2,6144]{2,1,0:T(2,128)(2,1)} %reshape.178), calls=%async_computation.3 | async-start | bytes 393216 | tf_op jit(solution)/shard_map/all_to_all | solution.py:101
  114.0 2.4 %copy-start.2 = (bf16[48,128,1,64]{1,3,0,2:T(8,128)(2,1)S(1)}, bf16[48,128,1,64]{1,3,0,2:T(8,128)(2,1)}, u32[]{:S(2)}) copy-start(bf16[48,128,1,64]{1,3,0,2:T(8,128)(2,1)} %get-tuple-element.141) | copy-start | bytes 2359300 | tf_op jit(solution)/shard_map/while
  118.8 2.4 %copy-start.2 = (bf16[48,128,1,64]{1,3,0,2:T(8,128)(2,1)S(1)}, bf16[48,128,1,64]{1,3,0,2:T(8,128)(2,1)}, u32[]{:S(2)}) copy-start(bf16[48,128,1,64]{1,3,0,2:T(8,128)(2,1)} %get-tuple-element.141) | copy-start | bytes 2359300 | tf_op jit(solution)/shard_map/while
  123.5 2.4 %copy-start.2 = (bf16[48,128,1,64]{1,3,0,2:T(8,128)(2,1)S(1)}, bf16[48,128,1,64]{1,3,0,2:T(8,128)(2,1)}, u32[]{:S(2)}) copy-start(bf16[48,128,1,64]{1,3,0,2:T(8,128)(2,1)} %get-tuple-element.141) | copy-start | bytes 2359300 | tf_op jit(solution)/shard_map/while
  128.2 2.4 %copy-start.2 = (bf16[48,128,1,64]{1,3,0,2:T(8,128)(2,1)S(1)}, bf16[48,128,1,64]{1,3,0,2:T(8,128)(2,1)}, u32[]{:S(2)}) copy-start(bf16[48,128,1,64]{1,3,0,2:T(8,128)(2,1)} %get-tuple-element.141) | copy-start | bytes 2359300 | tf_op jit(solution)/shard_map/while
  133.0 2.4 %copy-start.2 = (bf16[48,128,1,64]{1,3,0,2:T(8,128)(2,1)S(1)}, bf16[48,128,1,64]{1,3,0,2:T(8,128)(2,1)}, u32[]{:S(2)}) copy-start(bf16[48,128,1,64]{1,3,0,2:T(8,128)(2,1)} %get-tuple-element.141) | copy-start | bytes 2359300 | tf_op jit(solution)/shard_map/while
  137.7 2.4 %copy-start.2 = (bf16[48,128,1,64]{1,3,0,2:T(8,128)(2,1)S(1)}, bf16[48,128,1,64]{1,3,0,2:T(8,128)(2,1)}, u32[]{:S(2)}) copy-start(bf16[48,128,1,64]{1,3,0,2:T(8,128)(2,1)} %get-tuple-element.141) | copy-start | bytes 2359300 | tf_op jit(solution)/shard_map/while
  142.4 2.4 %copy-start.2 = (bf16[48,128,1,64]{1,3,0,2:T(8,128)(2,1)S(1)}, bf16[48,128,1,64]{1,3,0,2:T(8,128)(2,1)}, u32[]{:S(2)}) copy-start(bf16[48,128,1,64]{1,3,0,2:T(8,128)(2,1)} %get-tuple-element.141) | copy-start | bytes 2359300 | tf_op jit(solution)/shard_map/while
  147.2 2.4 %copy-start.2 = (bf16[48,128,1,64]{1,3,0,2:T(8,128)(2,1)S(1)}, bf16[48,128,1,64]{1,3,0,2:T(8,128)(2,1)}, u32[]{:S(2)}) copy-start(bf16[48,128,1,64]{1,3,0,2:T(8,128)(2,1)} %get-tuple-element.141) | copy-start | bytes 2359300 | tf_op jit(solution)/shard_map/while
  151.9 2.4 %copy-start.2 = (bf16[48,128,1,64]{1,3,0,2:T(8,128)(2,1)S(1)}, bf16[48,128,1,64]{1,3,0,2:T(8,128)(2,1)}, u32[]{:S(2)}) copy-start(bf16[48,128,1,64]{1,3,0,2:T(8,128)(2,1)} %get-tuple-element.141) | copy-start | bytes 2359300 | tf_op jit(solution)/shard_map/while
  156.7 2.4 %copy-start.2 = (bf16[48,128,1,64]{1,3,0,2:T(8,128)(2,1)S(1)}, bf16[48,128,1,64]{1,3,0,2:T(8,128)(2,1)}, u32[]{:S(2)}) copy-start(bf16[48,128,1,64]{1,3,0,2:T(8,128)(2,1)} %get-tuple-element.141) | copy-start | bytes 2359300 | tf_op jit(solution)/shard_map/while
  161.4 2.4 %copy-start.2 = (bf16[48,128,1,64]{1,3,0,2:T(8,128)(2,1)S(1)}, bf16[48,128,1,64]{1,3,0,2:T(8,128)(2,1)}, u32[]{:S(2)}) copy-start(bf16[48,128,1,64]{1,3,0,2:T(8,128)(2,1)} %get-tuple-element.141) | copy-start | bytes 2359300 | tf_op jit(solution)/shard_map/while
  166.2 2.4 %copy-start.2 = (bf16[48,128,1,64]{1,3,0,2:T(8,128)(2,1)S(1)}, bf16[48,128,1,64]{1,3,0,2:T(8,128)(2,1)}, u32[]{:S(2)}) copy-start(bf16[48,128,1,64]{1,3,0,2:T(8,128)(2,1)} %get-tuple-element.141) | copy-start | bytes 2359300 | tf_op jit(solution)/shard_map/while
  170.2 20.3 %copy-start.4 = (bf16[512,512]{1,0:T(8,128)(2,1)S(1)}, bf16[512,512]{1,0:T(8,128)(2,1)}, u32[]{:S(2)}) copy-start(bf16[512,512]{1,0:T(8,128)(2,1)} %param.18) | copy-start | bytes 1572868
Sparse Core Ops, SparseCore 0:
  10.7 93.0 all-gather.1
where the time goes:
time: 200 us; the launch traced here: 198 us
  waiting for transfers between devices  51.3 us (26%)
  matrix products  34.6 us (17%)
  blocking collectives  30.2 us (15%)
  local copies, waits for them, and re-layouts  27.5 us (14%)
  other arithmetic  23.4 us (12%)
  starting transfers between devices  17.3 us (9%)
  between operations  13.8 us (7%)
    all_gather x1, waiting for transfers between devices, fetch_all(): gathered = lax.all_gather(tile_kv, 'rows', axis=0, tiled=True)  20 us
    all_to_all x1, blocking collectives, shards(): lax.all_to_all(answer, 'cols', split_axis=1, concat_axis=2, tiled=True)  18.1 us
    dot_general x12, matrix products, one_block(): jnp.einsum('rchd,tkhd->rchtk', block_q, key_part, preferred_element_type=...  17.6 us
    all_to_all x1, waiting for transfers between devices, shards(): lax.all_to_all(keyvals, 'cols', split_axis=2, concat_axis=1, tiled=True)  12.4 us
    all_to_all x1, blocking collectives, shards(): lax.all_to_all(mixed_col, 'cols', split_axis=1, concat_axis=2, tiled=True)  12.2 us
    dot_general x12, matrix products, one_block(): jnp.einsum('rchtk,tkhd->rchd', tile_weights, val_part, preferred_element_...  11.6 us
    reduce_sum x12, other arithmetic, soft_weights(): jnp.sum(expo_vals, axis=axes, keepdims=True)  11.4 us
    all_to_all x1, starting transfers between devices, shards(): lax.all_to_all(queries, 'cols', split_axis=2, concat_axis=1, tiled=True)  10.3 us
  transfers between devices with their start and end apart: 4, of which 4 were waited for; matrix products, arithmetic and copies ran while one was open for 8% of the time, Pallas kernels for 0%

commit v1 on v0

--- a/solution.py
+++ b/solution.py
@@ -2,6 +2,18 @@
 import jax.numpy as jnp
 from jax import lax
 from jax.sharding import PartitionSpec as P
+
+
+def split_up(x, dim, size):
+    dims = x.shape
+    blocks = x.reshape(*dims[:dim], size, dims[dim] // size, *dims[dim + 1 :])
+    return jnp.moveaxis(blocks, dim, 0)
+
+
+def laid_out(blocks, dim):
+    blocks = jnp.moveaxis(blocks, 0, dim)
+    shape = blocks.shape
+    return blocks.reshape(*shape[:dim], shape[dim] * shape[dim + 1], *shape[dim + 2 :])
 
 
 def rms_scale(values, gain_vec):
@@ -100,7 +112,14 @@
     )
     asked_h = lax.all_to_all(asked_q, "cols", split_axis=2, concat_axis=1, tiled=True)
     answer = tile_attend(asked_h, fetched, key_mask, head_size)
-    answer_back = lax.all_to_all(answer, "cols", split_axis=1, concat_axis=2, tiled=True)
+    size, index = (lax.axis_size("cols"), lax.axis_index("cols"))
+    tiles = split_up(answer, 1, size)
+    outs = [tiles[index]]
+    for step in range(1, size):
+        sent = tiles[index ^ step]
+        outs.append(lax.ppermute(sent, "cols", [(i, i ^ step) for i in range(size)]))
+    tiles = jnp.stack(outs)[index ^ jnp.arange(size)]
+    answer_back = laid_out(tiles, 2)
     final_out = residual + project(answer_back, w_tile_out).reshape(residual.shape)
     return final_out.astype(jnp.bfloat16)
 

time: 200 us -> 214 us (1.070)
  starting transfers between devices: 17.3 us -> 48.3 us
  blocking collectives: 30.2 us -> 0 us
  waiting for transfers between devices: 51.3 us -> 64.4 us
  matrix products: 34.6 us -> 41.9 us
  local copies, waits for them, and re-layouts: 27.5 us -> 20.7 us
    all_to_all x2 -> x0, blocking collectives: 30.2 us -> none  [the longest x1 18.1 us: shards(): lax.all_to_all(answer, 'cols', split_axis=1, concat_axis=2, tiled=True)]
    ppermute x0 -> x7, starting transfers between devices: none -> 27.6 us  [shards(): lax.ppermute(sent, 'cols', [(i, i ^ step) for i in range(size)])]
    all_to_all x0 -> x1, waiting for transfers between devices: none -> 9.65 us  [shards(): lax.all_to_all(mixed_col, 'cols', split_axis=1, concat_axis=2, tiled=True)]
    dynamic_update_slice x12 -> x0, local copies, waits for them, and re-layouts: 7.7 us -> none  [tile_attend(): answer = lax.map(one_block, (q_blocks, m_blocks))]
    dot_general x12, matrix products: 11.6 us -> 18.9 us  [one_block(): jnp.einsum('rchtk,tkhd->rchd', tile_weights, val_part, preferred_element_...]
    ppermute x0 -> x7, waiting for transfers between devices: none -> 5.17 us  [shards(): lax.ppermute(sent, 'cols', [(i, i ^ step) for i in range(size)])]
    all_to_all x0 -> x1, starting transfers between devices: none -> 3.39 us  [shards(): lax.all_to_all(mixed_col, 'cols', split_axis=1, concat_axis=2, tiled=True)]
    unnamed x21 -> x33, local copies, waits for them, and re-layouts: 4.96 us -> 4.13 us
  transfers between devices with their start and end apart: 4 -> 12, of which waited for: 4 -> 7; matrix products, arithmetic and copies ran while one was open for 8% -> 8% of each run, Pallas kernels for 0% -> 0%
where the time goes in v1:
time: 214 us; the launch traced here: 213 us
  waiting for transfers between devices  64.4 us (30%)
  starting transfers between devices  48.3 us (23%)
  matrix products  41.9 us (20%)
  other arithmetic  23.4 us (11%)
  local copies, waits for them, and re-layouts  20.7 us (10%)
  between operations  14 us (7%)
    ppermute x7, starting transfers between devices, shards(): lax.ppermute(sent, 'cols', [(i, i ^ step) for i in range(size)])  27.6 us
    dot_general x12, matrix products, one_block(): jnp.einsum('rchtk,tkhd->rchd', tile_weights, val_part, preferred_element_...  18.9 us
    all_gather x1, waiting for transfers between devices, fetch_all(): gathered = lax.all_gather(tile_kv, 'rows', axis=0, tiled=True)  18.4 us
    dot_general x12, matrix products, one_block(): jnp.einsum('rchd,tkhd->rchtk', block_q, key_part, preferred_element_type=...  17.6 us
    all_to_all x1, waiting for transfers between devices, shards(): lax.all_to_all(keyvals, 'cols', split_axis=2, concat_axis=1, tiled=True)  12.4 us
    reduce_sum x12, other arithmetic, soft_weights(): jnp.sum(expo_vals, axis=axes, keepdims=True)  11.4 us
    all_to_all x1, starting transfers between devices, shards(): lax.all_to_all(queries, 'cols', split_axis=2, concat_axis=1, tiled=True)  10.3 us
    all_to_all x1, waiting for transfers between devices, shards(): lax.all_to_all(mixed_col, 'cols', split_axis=1, concat_axis=2, tiled=True)  9.65 us
  transfers between devices with their start and end apart: 12, of which 7 were waited for; matrix products, arithmetic and copies ran while one was open for 8% of the time, Pallas kernels for 0%

profile of v1, /device:TPU:8, one launch (start us, length us, event | category | flops | bytes accessed | tf_op | source)
XLA Modules:
  0.0 213.1 jit_solution(3804164555816505858)
XLA Ops:
  12.1 10.3 %all-to-all-start.1 = ((bf16[8,2,6144]{2,1,0:T(2,128)(2,1)}), bf16[8,2,6144]{2,1,0:T(2,128)(2,1)S(1)}, u32[]{:S(2)}, u32[]{:S(2)}) async-start(bf16[8,2,6144]{2,1,0:T(2,128)(2,1)} %reshape.209), calls=%async_computation.1 | async-start | bytes 393216 | tf_op jit(solution)/shard_map/all_to_all | solution.py:101
  24.1 8.8 %all-to-all-done.1 = bf16[8,2,6144]{2,1,0:T(2,128)(2,1)S(1)} async-done(((bf16[8,2,6144]{2,1,0:T(2,128)(2,1)}), bf16[8,2,6144]{2,1,0:T(2,128)(2,1)S(1)}, u32[]{:S(2)}, u32[]{:S(2)}) %all-to-all-start.1) | async-done | bytes 196640 | tf_op jit(solution)/shard_map/all_to_all | solution.py:101
  32.9 3.5 %all-to-all-start = ((bf16[48,4,8,128]{3,1,0,2:T(4,128)(2,1)}), bf16[48,4,8,128]{3,1,0,2:T(4,128)(2,1)S(1)}, u32[]{:S(2)}, u32[]{:S(2)}) async-start(bf16[48,4,8,128]{3,1,0,2:T(4,128)(2,1)} %pad_maximum_fusion), calls=%async_computation | async-start | bytes 786432 | tf_op jit(solution)/shard_map/all_to_all | solution.py:102
  37.0 12.4 %all-to-all-done = bf16[48,4,8,128]{3,1,0,2:T(4,128)(2,1)S(1)} async-done(((bf16[48,4,8,128]{3,1,0,2:T(4,128)(2,1)}), bf16[48,4,8,128]{3,1,0,2:T(4,128)(2,1)S(1)}, u32[]{:S(2)}, u32[]{:S(2)}) %all-to-all-start) | async-done | bytes 393248 | tf_op jit(solution)/shard_map/all_to_all | solution.py:102
  49.5 1.4 fusion.43
  50.9 1.6 fusion.29
  53.7 3.4 %all-to-all-start.2 = ((bf16[8,2,6144]{2,1,0:T(2,128)(2,1)}), bf16[8,2,6144]{2,1,0:T(2,128)(2,1)S(1)}, u32[]{:S(2)}, u32[]{:S(2)}) async-start(bf16[8,2,6144]{2,1,0:T(2,128)(2,1)} %reshape.211), calls=%async_computation.2 | async-start | bytes 393216 | tf_op jit(solution)/shard_map/all_to_all | solution.py:105
  57.1 9.6 %all-to-all-done.2 = bf16[8,2,6144]{2,1,0:T(2,128)(2,1)S(1)} async-done(((bf16[8,2,6144]{2,1,0:T(2,128)(2,1)}), bf16[8,2,6144]{2,1,0:T(2,128)(2,1)S(1)}, u32[]{:S(2)}, u32[]{:S(2)}) %all-to-all-start.2) | async-done | bytes 196640 | tf_op jit(solution)/shard_map/all_to_all | solution.py:105
  71.0 3.6 %all-to-all-start.3 = ((bf16[8,2,6144]{2,1,0:T(2,128)(2,1)}), bf16[8,2,6144]{2,1,0:T(2,128)(2,1)S(1)}, u32[]{:S(2)}, u32[]{:S(2)}) async-start(bf16[8,2,6144]{2,1,0:T(2,128)(2,1)} %reshape.213), calls=%async_computation.3 | async-start | bytes 393216 | tf_op jit(solution)/shard_map/all_to_all | solution.py:113
  74.7 9.4 %all-to-all-done.3 = bf16[8,2,6144]{2,1,0:T(2,128)(2,1)S(1)} async-done(((bf16[8,2,6144]{2,1,0:T(2,128)(2,1)}), bf16[8,2,6144]{2,1,0:T(2,128)(2,1)S(1)}, u32[]{:S(2)}, u32[]{:S(2)}) %all-to-all-start.3) | async-done | bytes 196640 | tf_op jit(solution)/shard_map/all_to_all | solution.py:113
  85.4 18.4 %all-gather.2.cloned.1.call-done = bf16[256,128,1,128]{3,1,2,0:T(8,128)(2,1)} async-done(((bf16[4,128,1,128]{3,1,2,0:T(8,128)(2,1)}), bf16[256,128,1,128]{3,1,2,0:T(8,128)(2,1)}) %all-gather.2.cloned.1.call-update) | async-done | bytes 8388624 | tf_op jit(solution)/shard_map/all_gather | solution.py:66
  103.8 4.2 %gather_fusion = bf16[48,128,128]{2,1,0:T(8,128)(2,1)S(1)} fusion(bf16[256,128,128]{2,1,0:T(8,128)(2,1)} %bitcast.243, s32[1024]{0:T(1024)S(1)} %pad_clamp_fusion.1), kind=kCustom, calls=%fused_computation | custom fusion | bytes 3145920 | tf_op jit(solution)/shard_map/jit(_take)/gather | solution.py:67
  108.2 1.9 fusion.41
  110.1 1.4 copy.101
  111.5 1.7 copy.100
  113.2 56.4 %while.10 = (s32[]{:T(128)}, bf16[12,4,32,1,64]{4,2,1,3,0:T(8,128)(2,1)}, s32[12,4,48]{2,1,0:T(4,128)}, bf16[12,4,32,1,64]{4,2,1,3,0:T(8,128)(2,1)}, bf16[48,128...) while((s32[]{:T(128)}, bf16[12,4,32,1,64]{4,2,1,3,0:T(8,128)(2,1)}, ...), condition=%wide.region_7.8_spmd, body=%wide.region_4.0_spmd.sunk | while | flops 210771904 | bytes 14225533 | solution.py:61
  113.9 1.5 fusion.61
  116.4 1.6 fusion.63
  118.6 1.5 fusion.61
  121.1 1.6 fusion.63
  123.3 1.5 fusion.61
  125.8 1.6 fusion.63
  128.0 1.5 fusion.61
  130.5 1.6 fusion.63
  132.7 1.5 fusion.61
  135.2 1.6 fusion.63
  137.4 1.5 fusion.61
  139.9 1.6 fusion.63
  142.1 1.5 fusion.61
  144.6 1.6 fusion.63
  146.8 1.5 fusion.61
  149.3 1.6 fusion.63
  151.5 1.5 fusion.61
  154.0 1.6 fusion.63
  156.2 1.5 fusion.61
  158.7 1.6 fusion.63
  160.9 1.5 fusion.61
  163.4 1.6 fusion.63
  165.6 1.5 fusion.61
  168.1 1.6 fusion.63
  170.9 3.5 %collective-permute-start = (bf16[48,4,1,64]{3,0,1,2:T(8,128)(2,1)S(1)}, bf16[48,4,1,64]{3,0,1,2:T(8,128)(2,1)S(1)}, u32[]{:S(2)}, u32[]{:S(2)}) collective-permute-start(bf16[48,4,1,64]{3,0,1,2:T(8,128)(2,1)S(1)} %bitcast.250), channel_id=1, source_target_pairs={{0,1},{1,0},{2,3},{3,2},{4,5},{5,4},{6,7},{7,6},{8,9},{9,8},{10,11... | collective-permute-start | bytes 73736 | tf_op jit(solution)/shard_map/ppermute | solution.py:120
  174.4 4.6 %collective-permute-start.1 = (bf16[48,4,1,64]{3,0,1,2:T(8,128)(2,1)S(1)}, bf16[48,4,1,64]{3,0,1,2:T(8,128)(2,1)S(1)}, u32[]{:S(2)}, u32[]{:S(2)}) collective-permute-start(bf16[48,4,1,64]{3,0,1,2:T(8,128)(2,1)S(1)} %bitcast.249), channel_id=1, source_target_pairs={{0,2},{1,3},{2,0},{3,1},{4,6},{5,7},{6,4},{7,5},{8,10},{9,11},{10,... | collective-permute-start | bytes 73736 | tf_op jit(solution)/shard_map/ppermute | solution.py:120
  179.1 2.0 collective-permute-start.2
  181.0 8.0 %collective-permute-start.3 = (bf16[48,4,1,64]{3,0,1,2:T(8,128)(2,1)S(1)}, bf16[48,4,1,64]{3,0,1,2:T(8,128)(2,1)S(1)}, u32[]{:S(2)}, u32[]{:S(2)}) collective-permute-start(bf16[48,4,1,64]{3,0,1,2:T(8,128)(2,1)S(1)} %bitcast.245), channel_id=1, source_target_pairs={{0,4},{1,5},{2,6},{3,7},{4,0},{5,1},{6,2},{7,3},{8,12},{9,13},{10,... | collective-permute-start | bytes 73736 | tf_op jit(solution)/shard_map/ppermute | solution.py:120
  189.0 1.9 collective-permute-start.4
  191.0 5.7 %collective-permute-start.5 = (bf16[48,4,1,64]{3,0,1,2:T(8,128)(2,1)S(1)}, bf16[48,4,1,64]{3,0,1,2:T(8,128)(2,1)S(1)}, u32[]{:S(2)}, u32[]{:S(2)}) collective-permute-start(bf16[48,4,1,64]{3,0,1,2:T(8,128)(2,1)S(1)} %bitcast.248), channel_id=1, source_target_pairs={{0,6},{1,7},{2,4},{3,5},{4,2},{5,3},{6,0},{7,1},{8,14},{9,15},{10,... | collective-permute-start | bytes 73736 | tf_op jit(solution)/shard_map/ppermute | solution.py:120
  196.7 1.9 collective-permute-start.6
  199.7 4.2 %collective-permute-done.6 = bf16[48,4,1,64]{3,0,1,2:T(8,128)(2,1)S(1)} collective-permute-done((bf16[48,4,1,64]{3,0,1,2:T(8,128)(2,1)S(1)}, bf16[48,4,1,64]{3,0,1,2:T(8,128)(2,1)S(1)}, u32[]{:S(2)}, u32[]{:S(2)}) %collective-permute-start.6) | collective-permute-done | bytes 24608 | tf_op jit(solution)/shard_map/ppermute | solution.py:120
  (129 shorter events, 39.0 us)
Async XLA Ops:
  6.5 3.1 %copy-start = (bf16[512,1536]{1,0:T(8,128)(2,1)S(1)}, bf16[512,1536]{1,0:T(8,128)(2,1)}, u32[]{:S(2)}) copy-start(bf16[512,1536]{1,0:T(8,128)(2,1)} %param.14) | copy-start | bytes 4718596
  6.5 97.2 %all-gather.2.cloned.1.call-start = ((), (), s32[]{:S(2)}) async-start(), calls=%async_computation.4 | async-start | bytes 8519680 | tf_op jit(solution)/shard_map/all_gather | solution.py:66
  12.1 20.8 %all-to-all-start.1 = ((bf16[8,2,6144]{2,1,0:T(2,128)(2,1)}), bf16[8,2,6144]{2,1,0:T(2,128)(2,1)S(1)}, u32[]{:S(2)}, u32[]{:S(2)}) async-start(bf16[8,2,6144]{2,1,0:T(2,128)(2,1)} %reshape.209), calls=%async_computation.1 | async-start | bytes 393216 | tf_op jit(solution)/shard_map/all_to_all | solution.py:101
  32.9 16.4 %all-to-all-start = ((bf16[48,4,8,128]{3,1,0,2:T(4,128)(2,1)}), bf16[48,4,8,128]{3,1,0,2:T(4,128)(2,1)S(1)}, u32[]{:S(2)}, u32[]{:S(2)}) async-start(bf16[48,4,8,128]{3,1,0,2:T(4,128)(2,1)} %pad_maximum_fusion), calls=%async_computation | async-start | bytes 786432 | tf_op jit(solution)/shard_map/all_to_all | solution.py:102
  49.5 7.6 %copy-start.6 = (s32[1,48]{1,0:T(1,128)S(1)}, s32[1,48]{1,0:T(1,128)}, u32[]{:S(2)}) copy-start(s32[1,48]{1,0:T(1,128)} %param.20) | copy-start | bytes 580
  50.9 16.7 %copy-start.1 = (bf16[48,4,512]{2,1,0:T(4,128)(2,1)S(1)}, bf16[48,4,512]{2,1,0:T(4,128)(2,1)}, u32[]{:S(2)}) copy-start(bf16[48,4,512]{2,1,0:T(4,128)(2,1)} %param.12) | copy-start | bytes 589828
  50.9 16.7 %copy-start.3 = (bf16[512,512]{1,0:T(8,128)(2,1)S(1)}, bf16[512,512]{1,0:T(8,128)(2,1)}, u32[]{:S(2)}) copy-start(bf16[512,512]{1,0:T(8,128)(2,1)} %param.15) | copy-start | bytes 1572868
  52.5 15.5 %copy-start.5 = (f32[512]{0:T(512)S(1)}, f32[512]{0:T(512)}, u32[]{:S(2)}) copy-start(f32[512]{0:T(512)} %param.16) | copy-start | bytes 6148
  53.7 13.1 %all-to-all-start.2 = ((bf16[8,2,6144]{2,1,0:T(2,128)(2,1)}), bf16[8,2,6144]{2,1,0:T(2,128)(2,1)S(1)}, u32[]{:S(2)}, u32[]{:S(2)}) async-start(bf16[8,2,6144]{2,1,0:T(2,128)(2,1)} %reshape.211), calls=%async_computation.2 | async-start | bytes 393216 | tf_op jit(solution)/shard_map/all_to_all | solution.py:105
  71.0 13.1 %all-to-all-start.3 = ((bf16[8,2,6144]{2,1,0:T(2,128)(2,1)}), bf16[8,2,6144]{2,1,0:T(2,128)(2,1)S(1)}, u32[]{:S(2)}, u32[]{:S(2)}) async-start(bf16[8,2,6144]{2,1,0:T(2,128)(2,1)} %reshape.213), calls=%async_computation.3 | async-start | bytes 393216 | tf_op jit(solution)/shard_map/all_to_all | solution.py:113
  113.9 2.4 %copy-start.2 = (bf16[48,128,1,64]{1,3,0,2:T(8,128)(2,1)S(1)}, bf16[48,128,1,64]{1,3,0,2:T(8,128)(2,1)}, u32[]{:S(2)}) copy-start(bf16[48,128,1,64]{1,3,0,2:T(8,128)(2,1)} %get-tuple-element.155) | copy-start | bytes 2359300 | tf_op jit(solution)/shard_map/while
  118.6 2.4 %copy-start.2 = (bf16[48,128,1,64]{1,3,0,2:T(8,128)(2,1)S(1)}, bf16[48,128,1,64]{1,3,0,2:T(8,128)(2,1)}, u32[]{:S(2)}) copy-start(bf16[48,128,1,64]{1,3,0,2:T(8,128)(2,1)} %get-tuple-element.155) | copy-start | bytes 2359300 | tf_op jit(solution)/shard_map/while
  123.3 2.4 %copy-start.2 = (bf16[48,128,1,64]{1,3,0,2:T(8,128)(2,1)S(1)}, bf16[48,128,1,64]{1,3,0,2:T(8,128)(2,1)}, u32[]{:S(2)}) copy-start(bf16[48,128,1,64]{1,3,0,2:T(8,128)(2,1)} %get-tuple-element.155) | copy-start | bytes 2359300 | tf_op jit(solution)/shard_map/while
  128.0 2.4 %copy-start.2 = (bf16[48,128,1,64]{1,3,0,2:T(8,128)(2,1)S(1)}, bf16[48,128,1,64]{1,3,0,2:T(8,128)(2,1)}, u32[]{:S(2)}) copy-start(bf16[48,128,1,64]{1,3,0,2:T(8,128)(2,1)} %get-tuple-element.155) | copy-start | bytes 2359300 | tf_op jit(solution)/shard_map/while
  132.7 2.4 %copy-start.2 = (bf16[48,128,1,64]{1,3,0,2:T(8,128)(2,1)S(1)}, bf16[48,128,1,64]{1,3,0,2:T(8,128)(2,1)}, u32[]{:S(2)}) copy-start(bf16[48,128,1,64]{1,3,0,2:T(8,128)(2,1)} %get-tuple-element.155) | copy-start | bytes 2359300 | tf_op jit(solution)/shard_map/while
  137.4 2.4 %copy-start.2 = (bf16[48,128,1,64]{1,3,0,2:T(8,128)(2,1)S(1)}, bf16[48,128,1,64]{1,3,0,2:T(8,128)(2,1)}, u32[]{:S(2)}) copy-start(bf16[48,128,1,64]{1,3,0,2:T(8,128)(2,1)} %get-tuple-element.155) | copy-start | bytes 2359300 | tf_op jit(solution)/shard_map/while
  142.1 2.4 %copy-start.2 = (bf16[48,128,1,64]{1,3,0,2:T(8,128)(2,1)S(1)}, bf16[48,128,1,64]{1,3,0,2:T(8,128)(2,1)}, u32[]{:S(2)}) copy-start(bf16[48,128,1,64]{1,3,0,2:T(8,128)(2,1)} %get-tuple-element.155) | copy-start | bytes 2359300 | tf_op jit(solution)/shard_map/while
  146.8 2.4 %copy-start.2 = (bf16[48,128,1,64]{1,3,0,2:T(8,128)(2,1)S(1)}, bf16[48,128,1,64]{1,3,0,2:T(8,128)(2,1)}, u32[]{:S(2)}) copy-start(bf16[48,128,1,64]{1,3,0,2:T(8,128)(2,1)} %get-tuple-element.155) | copy-start | bytes 2359300 | tf_op jit(solution)/shard_map/while
  151.5 2.4 %copy-start.2 = (bf16[48,128,1,64]{1,3,0,2:T(8,128)(2,1)S(1)}, bf16[48,128,1,64]{1,3,0,2:T(8,128)(2,1)}, u32[]{:S(2)}) copy-start(bf16[48,128,1,64]{1,3,0,2:T(8,128)(2,1)} %get-tuple-element.155) | copy-start | bytes 2359300 | tf_op jit(solution)/shard_map/while
  156.2 2.4 %copy-start.2 = (bf16[48,128,1,64]{1,3,0,2:T(8,128)(2,1)S(1)}, bf16[48,128,1,64]{1,3,0,2:T(8,128)(2,1)}, u32[]{:S(2)}) copy-start(bf16[48,128,1,64]{1,3,0,2:T(8,128)(2,1)} %get-tuple-element.155) | copy-start | bytes 2359300 | tf_op jit(solution)/shard_map/while
  160.9 2.4 %copy-start.2 = (bf16[48,128,1,64]{1,3,0,2:T(8,128)(2,1)S(1)}, bf16[48,128,1,64]{1,3,0,2:T(8,128)(2,1)}, u32[]{:S(2)}) copy-start(bf16[48,128,1,64]{1,3,0,2:T(8,128)(2,1)} %get-tuple-element.155) | copy-start | bytes 2359300 | tf_op jit(solution)/shard_map/while
  165.6 2.4 %copy-start.2 = (bf16[48,128,1,64]{1,3,0,2:T(8,128)(2,1)S(1)}, bf16[48,128,1,64]{1,3,0,2:T(8,128)(2,1)}, u32[]{:S(2)}) copy-start(bf16[48,128,1,64]{1,3,0,2:T(8,128)(2,1)} %get-tuple-element.155) | copy-start | bytes 2359300 | tf_op jit(solution)/shard_map/while
  169.6 35.5 %copy-start.4 = (bf16[512,512]{1,0:T(8,128)(2,1)S(1)}, bf16[512,512]{1,0:T(8,128)(2,1)}, u32[]{:S(2)}) copy-start(bf16[512,512]{1,0:T(8,128)(2,1)} %param.18) | copy-start | bytes 1572868
  170.9 20.1 %collective-permute-start = (bf16[48,4,1,64]{3,0,1,2:T(8,128)(2,1)S(1)}, bf16[48,4,1,64]{3,0,1,2:T(8,128)(2,1)S(1)}, u32[]{:S(2)}, u32[]{:S(2)}) collective-permute-start(bf16[48,4,1,64]{3,0,1,2:T(8,128)(2,1)S(1)} %bitcast.250), channel_id=1, source_target_pairs={{0,1},{1,0},{2,3},{3,2},{4,5},{5,4},{6,7},{7,6},{8,9},{9,8},{10,11... | collective-permute-start | bytes 73736 | tf_op jit(solution)/shard_map/ppermute | solution.py:120
  174.4 22.3 %collective-permute-start.1 = (bf16[48,4,1,64]{3,0,1,2:T(8,128)(2,1)S(1)}, bf16[48,4,1,64]{3,0,1,2:T(8,128)(2,1)S(1)}, u32[]{:S(2)}, u32[]{:S(2)}) collective-permute-start(bf16[48,4,1,64]{3,0,1,2:T(8,128)(2,1)S(1)} %bitcast.249), channel_id=1, source_target_pairs={{0,2},{1,3},{2,0},{3,1},{4,6},{5,7},{6,4},{7,5},{8,10},{9,11},{10,... | collective-permute-start | bytes 73736 | tf_op jit(solution)/shard_map/ppermute | solution.py:120
  179.1 19.6 %collective-permute-start.2 = (bf16[48,4,1,64]{3,0,1,2:T(8,128)(2,1)S(1)}, bf16[48,4,1,64]{3,0,1,2:T(8,128)(2,1)S(1)}, u32[]{:S(2)}, u32[]{:S(2)}) collective-permute-start(bf16[48,4,1,64]{3,0,1,2:T(8,128)(2,1)S(1)} %bitcast.246), channel_id=1, source_target_pairs={{0,3},{1,2},{2,1},{3,0},{4,7},{5,6},{6,5},{7,4},{8,11},{9,10},{10,... | collective-permute-start | bytes 73736 | tf_op jit(solution)/shard_map/ppermute | solution.py:120
  181.0 17.7 %collective-permute-start.3 = (bf16[48,4,1,64]{3,0,1,2:T(8,128)(2,1)S(1)}, bf16[48,4,1,64]{3,0,1,2:T(8,128)(2,1)S(1)}, u32[]{:S(2)}, u32[]{:S(2)}) collective-permute-start(bf16[48,4,1,64]{3,0,1,2:T(8,128)(2,1)S(1)} %bitcast.245), channel_id=1, source_target_pairs={{0,4},{1,5},{2,6},{3,7},{4,0},{5,1},{6,2},{7,3},{8,12},{9,13},{10,... | collective-permute-start | bytes 73736 | tf_op jit(solution)/shard_map/ppermute | solution.py:120
  189.0 9.7 %collective-permute-start.4 = (bf16[48,4,1,64]{3,0,1,2:T(8,128)(2,1)S(1)}, bf16[48,4,1,64]{3,0,1,2:T(8,128)(2,1)S(1)}, u32[]{:S(2)}, u32[]{:S(2)}) collective-permute-start(bf16[48,4,1,64]{3,0,1,2:T(8,128)(2,1)S(1)} %bitcast.244), channel_id=1, source_target_pairs={{0,5},{1,4},{2,7},{3,6},{4,1},{5,0},{6,3},{7,2},{8,13},{9,12},{10,... | collective-permute-start | bytes 73736 | tf_op jit(solution)/shard_map/ppermute | solution.py:120
  191.0 8.7 %collective-permute-start.5 = (bf16[48,4,1,64]{3,0,1,2:T(8,128)(2,1)S(1)}, bf16[48,4,1,64]{3,0,1,2:T(8,128)(2,1)S(1)}, u32[]{:S(2)}, u32[]{:S(2)}) collective-permute-start(bf16[48,4,1,64]{3,0,1,2:T(8,128)(2,1)S(1)} %bitcast.248), channel_id=1, source_target_pairs={{0,6},{1,7},{2,4},{3,5},{4,2},{5,3},{6,0},{7,1},{8,14},{9,15},{10,... | collective-permute-start | bytes 73736 | tf_op jit(solution)/shard_map/ppermute | solution.py:120
  196.7 7.2 %collective-permute-start.6 = (bf16[48,4,1,64]{3,0,1,2:T(8,128)(2,1)S(1)}, bf16[48,4,1,64]{3,0,1,2:T(8,128)(2,1)S(1)}, u32[]{:S(2)}, u32[]{:S(2)}) collective-permute-start(bf16[48,4,1,64]{3,0,1,2:T(8,128)(2,1)S(1)} %bitcast.247), channel_id=1, source_target_pairs={{0,7},{1,6},{2,5},{3,4},{4,3},{5,2},{6,1},{7,0},{8,15},{9,14},{10,... | collective-permute-start | bytes 73736 | tf_op jit(solution)/shard_map/ppermute | solution.py:120
Sparse Core Ops, SparseCore 0:
  10.7 93.0 all-gather.1
